TPU v7x, 512 devices: a whole 4x8x8 slice. The times are simulated.
512 devices in a mesh: ctx: 16 (over x, z_hi), row: 8 (over y), batch: 4 (over z_lo, core).
Axes of the slice: x: 4, y: 8, z: 8 (z_hi: 4, z_lo: 2; z = z_hi * 2 + z_lo), core: 2. Of those that a mesh axis runs over, the one named last changes fastest.
Arguments:
- queries: bfloat16 [12288, 5120], P(('batch', 'ctx'), 'row'), parts along dimension 0
- keys: bfloat16 [12288, 5120], P(('batch', 'ctx'), 'row'), parts along dimension 0
- values: bfloat16 [12288, 5120], P(('batch', 'ctx'), 'row'), parts along dimension 0, may hold values from -6 to 6
- gain_q: float32 [5120], P('row'), may hold values from 1.2 to 2.4
- gain_k: float32 [5120], P('row'), may hold values from 1.2 to 2.4
- clip_ids: int32 [12288], P(('batch', 'ctx')), parts along dimension 0, may hold values from 0 to 3, never falling along the last dimension, each value on 1 to 1920 neighbouring positions
- clip_grid: int32 [16, 2], P('batch'), parts along dimension 0, may hold values from 8 to 40
Outputs:
- attended: bfloat16 [12288, 5120], P(('batch', 'ctx'), 'row'), parts along dimension 0
There are 4 independent parts, one for each index of `batch`. A program takes and returns all parts, laid end to end along the dimension named above; an argument that names none is the same for every part. Nothing has to cross between parts.
Inputs may be any that keep to these rules, and one draw needn't show every extreme that they name: `clip_ids`: never falls along the tokens; each of the 4 clips has 1 to 1920 tokens, and one has exactly 1920.
All inputs are finite; a program needn't handle non-finite values.
Results may differ from a plain program's by a relative error of at most 0.012.
The roundings to bfloat16 on the way count: a program that leaves them out, or rounds other values in their place, can miss the bound.
Values may be sent and summed in bfloat16 or wider, within the bound.
A program may use at most 64 MiB of HBM per device.

v0:
```python
import math
import jax
import jax.numpy as jnp
from jax import lax
from jax.sharding import PartitionSpec as P

HD = 128
D = 5120
CLIPS = 4
EPSILON = 1e-06
NEGATIVE = -1e30
ROTARY_BASE = 10000.0
block_limit = 1024


def lookup(lookup_table, positions):
    labels = jnp.arange(lookup_table.shape[0], dtype=jnp.int32)
    return jnp.sum(
        jnp.where(positions[:, None] == labels[None, :], lookup_table[None, :], 0), axis=1
    )


def spin(matrix, offsets, clip_of, clip_grid, head_size):
    row_count = matrix.shape[0]
    sixth_part = head_size // 6
    first_dims = head_size - 4 * sixth_part
    first_freqs = 1.0 / ROTARY_BASE ** (
        jnp.arange(0, first_dims, 2, dtype=jnp.float32) / first_dims
    )
    other_freqs = 1.0 / ROTARY_BASE ** (
        jnp.arange(0, 2 * sixth_part, 2, dtype=jnp.float32) / (2 * sixth_part)
    )
    heights = lookup(clip_grid[:, 0], clip_of)
    widths = lookup(clip_grid[:, 1], clip_of)
    frame_pos = offsets // (heights * widths)
    line_pos = offsets // widths % heights
    column_pos = offsets % widths
    angles = jnp.concatenate(
        [
            frame_pos.astype(jnp.float32)[:, None] * first_freqs[None, :],
            line_pos.astype(jnp.float32)[:, None] * other_freqs[None, :],
            column_pos.astype(jnp.float32)[:, None] * other_freqs[None, :],
        ],
        axis=1,
    )
    cosine = jnp.repeat(jnp.cos(angles), 2, axis=1)
    sine_table = jnp.repeat(jnp.sin(angles), 2, axis=1)
    feature = jnp.arange(head_size, dtype=jnp.int32)
    is_even = (feature % 2 == 0)[None, None, :]
    head_view = matrix.reshape(row_count, -1, head_size)
    partner = jnp.where(is_even, -jnp.roll(head_view, -1, axis=2), jnp.roll(head_view, 1, axis=2))
    turned = head_view * cosine[:, None, :] + partner * sine_table[:, None, :]
    return turned.reshape(row_count, -1)


def on_device(queries, keys, values, gain_q, gain_k, clip_ids, clip_grid):
    rows_here, width_here = queries.shape
    heads_here = width_here // HD
    score_scale = 1.0 / math.sqrt(HD)
    query_wide = queries.astype(jnp.float32)
    key_wide = keys.astype(jnp.float32)
    squares = lax.psum(
        (jnp.sum(query_wide * query_wide, axis=1), jnp.sum(key_wide * key_wide, axis=1)), "row"
    )
    query_scale = lax.rsqrt(squares[0] / D + EPSILON)
    key_scale = lax.rsqrt(squares[1] / D + EPSILON)
    labels = jnp.arange(CLIPS, dtype=jnp.int32)
    local_counts = jnp.sum((clip_ids[:, None] == labels[None, :]).astype(jnp.int32), axis=0)
    totals = lax.psum(local_counts, "ctx")
    starts = jnp.cumsum(totals) - totals
    first_row = lax.axis_index("ctx") * rows_here
    offsets = first_row + jnp.arange(rows_here, dtype=jnp.int32) - lookup(starts, clip_ids)
    query_rot = spin(
        query_wide * query_scale[:, None] * gain_q[None, :], offsets, clip_ids, clip_grid, HD
    ).astype(jnp.bfloat16)
    query_heads = query_rot.reshape(rows_here, heads_here, HD)
    key_send = spin(
        key_wide * key_scale[:, None] * gain_k[None, :], offsets, clip_ids, clip_grid, HD
    ).astype(jnp.bfloat16)
    initial = (
        jnp.full((heads_here, rows_here), NEGATIVE, jnp.float32),
        jnp.zeros((heads_here, rows_here), jnp.float32),
        jnp.zeros((rows_here, heads_here, HD), jnp.float32),
    )
    running = initial
    piece_start = jnp.int32(0)
    key_piece = lax.all_gather(key_send, "ctx", axis=0, tiled=True)
    value_piece = lax.all_gather(values, "ctx", axis=0, tiled=True)
    row_count = key_piece.shape[0]
    block_rows = min(row_count, block_limit)
    for block_first in range(0, row_count, block_rows):
        block_size = min(block_rows, row_count - block_first)
        fold_key_rows = key_piece[block_first : block_first + block_size]
        fold_value_rows = value_piece[block_first : block_first + block_size]
        key_index = piece_start + block_first + jnp.arange(fold_key_rows.shape[0], dtype=jnp.int32)
        key_key_clips = (
            jnp.sum((starts[None, :] <= key_index[:, None]).astype(jnp.int32), axis=1) - 1
        )
        peak_old, total_old, summed_old = running
        key_view = fold_key_rows.reshape(fold_key_rows.shape[0], heads_here, HD)
        value_view = fold_value_rows.reshape(fold_value_rows.shape[0], heads_here, HD)
        scores = (
            jnp.einsum("qhd,khd->hqk", query_heads, key_view, preferred_element_type=jnp.float32)
            * score_scale
        )
        same = clip_ids[:, None] == key_key_clips[None, :]
        masked = jnp.where(same[None, :, :], scores, NEGATIVE)
        peak_new = jnp.maximum(peak_old, jnp.max(masked, axis=2))
        weights = jnp.where(same[None, :, :], jnp.exp(masked - peak_new[:, :, None]), 0.0)
        factor = jnp.exp(peak_old - peak_new)
        total_new = total_old * factor + jnp.sum(weights, axis=2)
        summed = summed_old * jnp.transpose(factor)[:, :, None] + jnp.einsum(
            "hqk,khd->qhd",
            weights.astype(jnp.bfloat16),
            value_view,
            preferred_element_type=jnp.float32,
        )
        running = (peak_new, total_new, summed)
    attended = running[2] / jnp.transpose(running[1])[:, :, None]
    return attended.reshape(rows_here, width_here).astype(jnp.bfloat16)


def solution(mesh):
    in_specs = (
        P(("batch", "ctx"), "row"),
        P(("batch", "ctx"), "row"),
        P(("batch", "ctx"), "row"),
        P("row"),
        P("row"),
        P(("batch", "ctx")),
        P("batch", None),
    )
    out_specs = P(("batch", "ctx"), "row")
    return jax.shard_map(
        on_device, mesh=mesh, in_specs=in_specs, out_specs=out_specs, check_vma=False
    )
```

profile of v0, /device:TPU:1, one launch (start us, length us, event | category | flops | bytes accessed | tf_op | source)
XLA Modules:
  0.0 213.5 jit_solution(10910715953771418640)
XLA Ops:
  6.5 0.7 all-gather.5.cloned.1.call-update
  7.3 0.8 convert_reduce_fusion.3
  8.1 20.5 %psum.21 = s32[4]{0:T(128)S(1)} all-reduce(s32[4]{0:T(128)S(1)} %convert_reduce_fusion.3), channel_id=1, replica_groups=mesh['ctx'=16,'row'=8,'batch'=4] {'ctx'}, use_global_device_ids=true, to_apply=%region_1.0 | all-reduce | flops 4 | bytes 32 | tf_op jit(solution)/shard_map/psum | solution.py:69
  28.6 0.2 reduce-window.9
  28.8 0.8 slice_bitcast_fusion
  29.6 0.8 select_reduce_fusion.1
  30.4 0.3 fusion.65
  30.6 0.1 broadcast_multiply_fusion.2
  30.8 0.3 fusion.57
  31.1 0.1 mul.208
  31.2 0.1 mul.212
  31.3 1.1 copy.45
  32.5 1.1 copy.46
  33.6 0.1 fusion.48
  33.7 0.1 fusion.50
  33.8 15.1 %all-reduce = (f32[192]{0:T(256)S(1)}, f32[192]{0:T(256)S(1)}) all-reduce(f32[192]{0:T(256)S(1)} %fusion.48, f32[192]{0:T(256)S(1)} %fusion.50), channel_id=1, replica_groups=mesh['ctx'=16,'row'=8,'batch'=4] {'row'}, use_global_device_ids=true, to_apply=%region_5.0 | all-reduce | flops 384 | bytes 3072 | tf_op jit(solution)/shard_map/psum | solution.py:62
  49.0 0.8 fusion.49
  49.8 0.1 fusion.85
  50.0 0.1 pad_maximum_fusion
  50.1 0.1 fusion.51
  50.3 0.1 fusion.83
  50.5 0.1 pad_maximum_fusion.1
  50.6 0.1 copy-done.4
  50.7 0.4 fusion.55
  51.2 0.9 copy.47
  52.1 0.1 convert_reduce_fusion
  52.2 0.4 broadcast_compare_fusion
  52.6 44.7 %all-gather.5.cloned.1.call-done = bf16[3072,640]{1,0:T(8,128)(2,1)} async-done(((bf16[192,640]{1,0:T(8,128)(2,1)}), bf16[3072,640]{1,0:T(8,128)(2,1)}) %all-gather.5.cloned.1.call-update) | async-done | bytes 3932176 | tf_op jit(solution)/shard_map/all_gather | solution.py:88
  97.3 4.0 %fusion.81 = (bf16[1024,640]{1,0:T(8,128)(2,1)S(1)}, bf16[1024,640]{1,0:T(8,128)(2,1)}, bf16[1024,640]{1,0:T(8,128)(2,1)}) fusion(bf16[3072,640]{1,0:T(8,128)(2,1)} %all-gather.5.cloned.1.call-done), kind=kLoop, calls=%fused_computation.121 | loop fusion | bytes 7864320 | tf_op jit(solution)/shard_map/slice | solution.py:94
  101.3 1.5 copy.79
  102.8 76.7 %all-gather.3.cloned.1.call-done = bf16[3072,640]{1,0:T(8,128)(2,1)} async-done(((bf16[192,640]{1,0:T(8,128)(2,1)}), bf16[3072,640]{1,0:T(8,128)(2,1)}) %all-gather.3.cloned.1.call-update) | async-done | bytes 3932176 | tf_op jit(solution)/shard_map/all_gather | solution.py:87
  179.5 3.9 %fusion.82 = (bf16[1024,640]{1,0:T(8,128)(2,1)S(1)}, bf16[1024,640]{1,0:T(8,128)(2,1)}, bf16[1024,640]{1,0:T(8,128)(2,1)}) fusion(bf16[3072,640]{1,0:T(8,128)(2,1)} %all-gather.3.cloned.1.call-done), kind=kLoop, calls=%fused_computation.122 | loop fusion | bytes 7864320 | tf_op jit(solution)/shard_map/slice | solution.py:93
  183.4 0.6 copy.78
  184.1 1.6 copy.76
  185.7 2.5 %copy.74 = bf16[1024,640]{0,1:T(8,128)(2,1)} copy(bf16[1024,640]{1,0:T(8,128)(2,1)} %get-tuple-element.22) | data formatting | bytes 2621440
  188.2 2.5 %copy.77 = bf16[1024,640]{0,1:T(8,128)(2,1)} copy(bf16[1024,640]{1,0:T(8,128)(2,1)} %get-tuple-element.18) | data formatting | bytes 2621440
  190.7 2.5 %copy.75 = bf16[1024,640]{0,1:T(8,128)(2,1)} copy(bf16[1024,640]{1,0:T(8,128)(2,1)} %get-tuple-element.19) | data formatting | bytes 2621440
  193.2 2.4 %fusion = (f32[5,192]{1,0:T(8,128)S(1)}, f32[5,192,1024]{2,1,0:T(8,128)S(1)}) fusion(pred[192,1024]{1,0:T(8,128)(4,1)S(1)} %get-tuple-element.43, bf16[192,5,128]{0,2,1:T(8,128)(2,1)S(1)} %bitcast.131, bf16[1024,5,128]{0,2,1:T(8,128)(2,1)} %bitcast.136), kind=kOutput, calls=%fused_computation.6 | convolution fusion | flops 254606400 | bytes 5689088 | tf_op jit(solution)/shard_map/qhd,khd->hqk/dot_general | solution.py:103
  195.6 1.1 fusion.1
  196.6 1.1 fusion.2
  197.7 1.3 fusion.7
  199.0 1.3 fusion.5
  200.3 1.3 fusion.3
  201.6 1.3 fusion.39
  202.9 1.3 fusion.33
  204.3 1.3 fusion.45
  205.6 0.2 copy.63
  205.8 0.9 copy.64
  (33 shorter events, 0.5 us)
Async XLA Ops:
  6.5 90.7 %all-gather.5.cloned.1.call-start = ((), (), s32[]{:S(2)}) async-start(), calls=%async_computation.1 | async-start | bytes 4177920 | tf_op jit(solution)/shard_map/all_gather | solution.py:88
  7.3 172.2 %all-gather.3.cloned.1.call-start = ((), (), s32[]{:S(2)}) async-start(), calls=%async_computation | async-start | bytes 4177920 | tf_op jit(solution)/shard_map/all_gather | solution.py:87
  31.3 18.8 %copy-start.3 = (f32[640]{0:T(1024)S(1)}, f32[640]{0:T(1024)}, u32[]{:S(2)}) copy-start(f32[640]{0:T(1024)} %param.11) | copy-start | bytes 7684
  50.0 0.7 copy-start.4
  50.4 1.8 copy-start.5
  199.0 2.6 %copy-start.2 = (bf16[1024,640]{0,1:T(8,128)(2,1)S(1)}, bf16[1024,640]{0,1:T(8,128)(2,1)}, u32[]{:S(2)}) copy-start(bf16[1024,640]{0,1:T(8,128)(2,1)} %copy.75) | copy-start | bytes 3932164
  201.6 1.3 copy-start.1
  202.9 1.3 copy-start
Sparse Core Ops, SparseCore 0:
  10.4 86.8 all-gather.4
  100.3 79.1 all-gather.2
where the time goes:
time: 214 us
  waiting for transfers between devices  122 us (57%)
  blocking collectives  35.7 us (17%)
  local copies, waits for them, and re-layouts  24.8 us (12%)
  between operations  13.8 us (6%)
  other arithmetic  8.73 us (4%)
  matrix products  8.44 us (4%)
    all_gather x1, waiting for transfers between devices, on_device(): key_piece = lax.all_gather(key_send, 'ctx', axis=0, tiled=True)  76.7 us
    all_gather x1, waiting for transfers between devices, on_device(): value_piece = lax.all_gather(values, 'ctx', axis=0, tiled=True)  44.7 us
    psum x1, blocking collectives, on_device(): totals = lax.psum(local_counts, 'ctx')  20.5 us
    psum x1, blocking collectives, on_device(): lax.psum((jnp.sum(query_wide * query_wide, axis=1), jnp.sum(key_wide * ke...  15.1 us
    unnamed x20, local copies, waits for them, and re-layouts  13.6 us
    dot_general x3, matrix products, on_device(): jnp.einsum('qhd,khd->hqk', query_heads, key_view, preferred_element_type=...  4.46 us
  transfers between devices with their start and end apart: 2, of which 2 were waited for; matrix products, arithmetic and copies ran while one was open for 7% of the time, Pallas kernels for 0%

commit v1 on v0

--- a/solution.py
+++ b/solution.py
@@ -85,7 +85,8 @@
     running = initial
     piece_start = jnp.int32(0)
     key_piece = lax.all_gather(key_send, "ctx", axis=0, tiled=True)
-    value_piece = lax.all_gather(values, "ctx", axis=0, tiled=True)
+    sent = jnp.stack([values] * lax.axis_size("ctx"))
+    value_piece = jnp.concatenate(lax.all_to_all(sent, "ctx", 0, 0), axis=0)
     row_count = key_piece.shape[0]
     block_rows = min(row_count, block_limit)
     for block_first in range(0, row_count, block_rows):

time: 214 us -> 244 us (1.14)
  blocking collectives: 35.7 us -> 90.1 us
  waiting for transfers between devices: 122 us -> 81.3 us
  starting transfers between devices: 0.04 us -> 13.6 us
  other arithmetic: 8.73 us -> 11.7 us
    psum x1, blocking collectives: 20.5 us -> 74.6 us  [on_device(): totals = lax.psum(local_counts, 'ctx')]
    all_gather x1 -> x0, waiting for transfers between devices: 44.7 us -> none  [on_device(): value_piece = lax.all_gather(values, 'ctx', axis=0, tiled=True)]
    all_to_all x0 -> x1, starting transfers between devices: none -> 13.6 us  [on_device(): value_piece = jnp.concatenate(lax.all_to_all(sent, 'ctx', 0, 0), axis=0)]
    unnamed x20 -> x25, local copies, waits for them, and re-layouts: 13.6 us -> 4.21 us
    slice x1 -> x4, local copies, waits for them, and re-layouts: 4.03 us -> 10.5 us  [on_device(): fold_value_rows = value_piece[block_first:block_first + block_size]]
    all_gather x1, waiting for transfers between devices: 76.7 us -> 81.2 us  [on_device(): key_piece = lax.all_gather(key_send, 'ctx', axis=0, tiled=True)]
    another operation x0 -> x1, local copies, waits for them, and re-layouts: none -> 3.3 us  [on_device(): sent = jnp.stack([values] * lax.axis_size('ctx'))]
    concatenate x2, other arithmetic: 0.14 us -> 2.98 us  [spin(): jnp.roll(head_view, 1, axis=2)]
  transfers between devices with their start and end apart: 2 -> 2, of which waited for: 2 -> 1; matrix products, arithmetic and copies ran while one was open for 7% -> 7% of each run, Pallas kernels for 0% -> 0%
where the time goes in v1:
time: 244 us
  blocking collectives  90.1 us (37%)
  waiting for transfers between devices  81.3 us (33%)
  local copies, waits for them, and re-layouts  24.8 us (10%)
  between operations  13.8 us (6%)
  starting transfers between devices  13.6 us (6%)
  other arithmetic  11.7 us (5%)
  matrix products  8.4 us (3%)
    all_gather x1, waiting for transfers between devices, on_device(): key_piece = lax.all_gather(key_send, 'ctx', axis=0, tiled=True)  81.2 us
    psum x1, blocking collectives, on_device(): totals = lax.psum(local_counts, 'ctx')  74.6 us
    psum x1, blocking collectives, on_device(): lax.psum((jnp.sum(query_wide * query_wide, axis=1), jnp.sum(key_wide * ke...  15.5 us
    all_to_all x1, starting transfers between devices, on_device(): value_piece = jnp.concatenate(lax.all_to_all(sent, 'ctx', 0, 0), axis=0)  13.6 us
    slice x4, local copies, waits for them, and re-layouts, on_device(): fold_value_rows = value_piece[block_first:block_first + block_size]  10.5 us
  transfers between devices with their start and end apart: 2, of which 1 were waited for; matrix products, arithmetic and copies ran while one was open for 7% of the time, Pallas kernels for 0%

profile of v1, /device:TPU:1, one launch (start us, length us, event | category | flops | bytes accessed | tf_op | source)
XLA Modules:
  0.0 243.6 jit_solution(1093172625096793564)
XLA Ops:
  6.5 3.3 %stack.2 = bf16[16,192,640]{2,1,0:T(8,128)(2,1)} broadcast(bf16[192,640]{1,0:T(8,128)(2,1)} %param.9), dimensions={1,2} | broadcast | bytes 4177920 | tf_op jit(solution)/shard_map/stack | solution.py:88
  9.8 13.6 %all-to-all-start = ((bf16[16,192,640]{2,1,0:T(8,128)(2,1)}), bf16[16,192,640]{2,1,0:T(8,128)(2,1)}, u32[]{:S(2)}, u32[]{:S(2)}) async-start(bf16[16,192,640]{2,1,0:T(8,128)(2,1)} %stack.2), calls=%async_computation | async-start | bytes 7864320 | tf_op jit(solution)/shard_map/all_to_all | solution.py:89
  23.5 0.2 copy.62
  23.7 0.2 copy.61
  23.9 0.1 fusion.48
  24.0 0.1 fusion.50
  24.1 15.5 %all-reduce = (f32[192]{0:T(256)S(1)}, f32[192]{0:T(256)S(1)}) all-reduce(f32[192]{0:T(256)S(1)} %fusion.48, f32[192]{0:T(256)S(1)} %fusion.50), channel_id=1, replica_groups=mesh['ctx'=16,'row'=8,'batch'=4] {'row'}, use_global_device_ids=true, to_apply=%region_5.0 | all-reduce | flops 384 | bytes 3072 | tf_op jit(solution)/shard_map/psum | solution.py:62
  39.6 0.2 fusion.51
  39.8 1.0 fusion.83
  40.8 0.1 fusion.49
  41.0 0.1 fusion.85
  41.1 0.1 convert_reduce_fusion.3
  41.2 74.6 %psum.21 = s32[4]{0:T(128)S(1)} all-reduce(s32[4]{0:T(128)S(1)} %convert_reduce_fusion.3), channel_id=1, replica_groups=mesh['ctx'=16,'row'=8,'batch'=4] {'ctx'}, use_global_device_ids=true, to_apply=%region_1.0 | all-reduce | flops 4 | bytes 32 | tf_op jit(solution)/shard_map/psum | solution.py:69
  115.8 0.2 reduce-window.9
  116.0 2.0 pad_maximum_fusion.1
  118.1 0.9 maximum_negate_fusion.1
  119.0 0.1 select_reduce_fusion.1
  119.1 0.3 fusion.65
  119.4 0.1 broadcast_multiply_fusion.2
  119.4 0.9 pad_maximum_fusion
  120.4 0.1 broadcast_multiply_fusion.1
  120.4 0.3 fusion.57
  120.8 0.1 mul.212
  120.9 0.1 mul.208
  121.1 1.7 fusion.55
  122.8 0.9 copy.63
  123.7 0.1 convert_reduce_fusion
  123.9 0.4 broadcast_compare_fusion
  124.2 3.9 %fusion.81 = (bf16[1024,640]{1,0:T(8,128)(2,1)}, bf16[1024,640]{1,0:T(8,128)(2,1)}, bf16[1024,640]{1,0:T(8,128)(2,1)S(1)}) fusion(bf16[3072,640]{1,0:T(8,128)(2,1)} %bitcast.16), kind=kLoop, calls=%fused_computation.121 | loop fusion | bytes 7864320 | tf_op jit(solution)/shard_map/slice | solution.py:95
  128.2 1.6 copy.67
  129.7 81.2 %all-gather.2.cloned.1.call-done = bf16[3072,640]{1,0:T(8,128)(2,1)} async-done(((bf16[192,640]{1,0:T(8,128)(2,1)}), bf16[3072,640]{1,0:T(8,128)(2,1)}) %all-gather.2.cloned.1.call-update) | async-done | bytes 3932176 | tf_op jit(solution)/shard_map/all_gather | solution.py:87
  211.0 3.5 %fusion.82 = (bf16[1024,640]{1,0:T(8,128)(2,1)S(1)}, bf16[1024,640]{1,0:T(8,128)(2,1)}, bf16[1024,640]{1,0:T(8,128)(2,1)S(1)}) fusion(bf16[3072,640]{1,0:T(8,128)(2,1)} %all-gather.2.cloned.1.call-done), kind=kLoop, calls=%fused_computation.122 | loop fusion | bytes 7864320 | tf_op jit(solution)/shard_map/slice | solution.py:94
  214.5 1.5 copy.90
  216.1 0.6 copy.92
  216.7 1.6 copy.91
  218.3 2.5 %copy.72 = bf16[1024,640]{0,1:T(8,128)(2,1)} copy(bf16[1024,640]{1,0:T(8,128)(2,1)} %get-tuple-element.18) | data formatting | bytes 2621440 | tf_op jit(solution)/shard_map/slice | solution.py:95
  220.8 2.5 %copy.77 = bf16[1024,640]{0,1:T(8,128)(2,1)} copy(bf16[1024,640]{1,0:T(8,128)(2,1)} %get-tuple-element.17) | data formatting | bytes 2621440 | tf_op jit(solution)/shard_map/slice | solution.py:95
  223.3 2.4 fusion
  225.7 1.1 fusion.2
  226.8 1.1 fusion.1
  227.8 1.3 fusion.7
  229.1 1.3 fusion.5
  230.4 1.3 fusion.3
  231.7 1.3 fusion.39
  233.1 1.3 fusion.33
  234.4 1.3 fusion.45
  235.7 0.2 copy.79
  235.9 0.9 copy.80
  (41 shorter events, 0.4 us)
Async XLA Ops:
  9.8 13.7 %copy-start.4 = (bf16[192,640]{1,0:T(8,128)(2,1)S(1)}, bf16[192,640]{1,0:T(8,128)(2,1)}, u32[]{:S(2)}) copy-start(bf16[192,640]{1,0:T(8,128)(2,1)} %param.8) | copy-start | bytes 737284
  9.8 13.9 %copy-start.5 = (bf16[192,640]{1,0:T(8,128)(2,1)S(1)}, bf16[192,640]{1,0:T(8,128)(2,1)}, u32[]{:S(2)}) copy-start(bf16[192,640]{1,0:T(8,128)(2,1)} %param.7) | copy-start | bytes 737284
  9.8 29.8 %copy-start.6 = (f32[640]{0:T(1024)S(1)}, f32[640]{0:T(1024)}, u32[]{:S(2)}) copy-start(f32[640]{0:T(1024)} %param.11) | copy-start | bytes 7684
  9.8 114.4 %all-to-all-start = ((bf16[16,192,640]{2,1,0:T(8,128)(2,1)}), bf16[16,192,640]{2,1,0:T(8,128)(2,1)}, u32[]{:S(2)}, u32[]{:S(2)}) async-start(bf16[16,192,640]{2,1,0:T(8,128)(2,1)} %stack.2), calls=%async_computation | async-start | bytes 7864320 | tf_op jit(solution)/shard_map/all_to_all | solution.py:89
  23.4 17.4 %copy-start.7 = (f32[640]{0:T(1024)S(1)}, f32[640]{0:T(1024)}, u32[]{:S(2)}) copy-start(f32[640]{0:T(1024)} %param.10) | copy-start | bytes 7684
  23.4 187.5 %all-gather.2.cloned.1.call-start = ((), (), s32[]{:S(2)}) async-start(), calls=%async_computation.1 | async-start | bytes 4177920 | tf_op jit(solution)/shard_map/all_gather | solution.py:87
  23.9 17.2 %copy-start.8 = (s32[192]{0:T(256)S(1)}, s32[192]{0:T(256)}, u32[]{:S(2)}) copy-start(s32[192]{0:T(256)} %param.12) | copy-start | bytes 2308
  23.9 92.1 %copy-start.9 = (s32[4,2]{0,1:T(2,128)S(1)}, s32[4,2]{0,1:T(2,128)}, u32[]{:S(2)}) copy-start(s32[4,2]{0,1:T(2,128)} %param.13) | copy-start | bytes 100
  119.0 2.1 copy-start
  229.1 2.6 %copy-start.1 = (bf16[1024,640]{0,1:T(8,128)(2,1)S(1)}, bf16[1024,640]{0,1:T(8,128)(2,1)}, u32[]{:S(2)}) copy-start(bf16[1024,640]{0,1:T(8,128)(2,1)} %copy.67) | copy-start | bytes 3932164
  231.7 1.3 copy-start.3
  233.1 1.3 copy-start.2
Sparse Core Ops, SparseCore 0:
  123.8 87.1 all-gather.1
